TPU v7x, 128 devices: a whole 4x4x4 slice. The times are simulated.
128 devices in a mesh: row: 8 (over z, core), col: 16 (over y, x).
Axes of the slice: x: 4, y: 4, z: 4, core: 2. Of those that a mesh axis runs over, the one named last changes fastest.
Arguments:
- amp_tiles: float32 [16, 32, 256, 256], P('row', 'col'), may hold values from -6 to 6
- int_tiles: float32 [32, 32, 256, 256], P('col', 'row'), may hold values from -0.125 to 0.125
- resid_init: float32 [16, 32, 256, 256], P('row', 'col'), may hold values from -6 to 6
- triples: int32 [8, 16, 3, 32], P('row', 'col'), may hold values from 0 to 1023, as said below
Outputs:
- resid_out: float32 [16, 32, 256, 256], P('row', 'col')
Inputs may be any that keep to these rules, and one draw needn't show every extreme that they name: Each triple names tiles (i, j), (j, k), (i, k) with one i, j, k. The amplitude tile of every triple on device (r, c) is one that device holds. For every device and every column index q, exactly 2 distinct residual tiles held at (r, q) are named by that device's triples, each by exactly one of that device's triples. No triple is listed twice; the order of triples on a device is arbitrary.
All inputs are finite; a program needn't handle non-finite values.
Results may differ from a plain program's by a relative error of at most 0.0001.
Values sent between devices are 32-bit elements; how exact they have to be, the bound alone decides.
No kernel may reach another device: no remote copies, remote signals or barrier semaphores. Data moves between devices by JAX's collectives and lax.ppermute only.
A program may use at most 128 MiB of HBM per device.

v0:
```python
import jax
import jax.numpy as jnp
from jax import lax
from jax.sharding import PartitionSpec as P


def on_device(amp_tiles, int_tiles, resid_init, triples):
    occ_blocks = amp_tiles.shape[0]
    vir_blocks = amp_tiles.shape[1]
    width = amp_tiles.shape[2]
    own_k = resid_init.shape[1]
    col_count = lax.axis_size("col")
    all_k = own_k * col_count
    all_j = vir_blocks * col_count
    row_place = lax.axis_index("row")
    col_place = lax.axis_index("col")
    listing = triples[0, 0]
    amp_ids = listing[0]
    int_ids = listing[1]
    res_ids = listing[2]
    amp_occ = amp_ids // all_j - row_place * occ_blocks
    amp_vir = amp_ids % all_j - col_place * vir_blocks
    int_vir = int_ids // all_k - col_place * vir_blocks
    int_col = int_ids % all_k
    res_occ = res_ids // all_k - row_place * occ_blocks
    res_col = res_ids % all_k
    amp_index = amp_occ * vir_blocks + amp_vir
    int_index = int_vir * all_k + int_col
    gathered = lax.all_gather(int_tiles, "row", axis=1, tiled=True)
    amp_flat = amp_tiles.reshape(-1, width, width)
    int_flat = gathered.reshape(-1, width, width)
    target = res_occ * all_k + res_col
    slots_total = occ_blocks * all_k
    block = 8

    def add_block(partial_value, pieces):
        amp_pick, int_pick, target_pick = pieces
        products = jnp.einsum(
            "bxy,byz->bxz",
            amp_flat[amp_pick],
            int_flat[int_pick],
            precision=lax.Precision.HIGHEST,
            preferred_element_type=jnp.float32,
        )
        return (partial_value.at[target_pick].add(products), None)

    start = jnp.zeros((slots_total, width, width), jnp.float32)
    pieces = (amp_index.reshape(-1, block), int_index.reshape(-1, block), target.reshape(-1, block))
    partial_value, _ = lax.scan(add_block, start, pieces)
    summed = lax.psum_scatter(
        partial_value.reshape(occ_blocks, all_k, width, width),
        "col",
        scatter_dimension=1,
        tiled=True,
    )
    return resid_init + summed


def solution(mesh):
    return jax.shard_map(
        on_device,
        mesh=mesh,
        in_specs=(
            P("row", "col", None, None),
            P("col", "row", None, None),
            P("row", "col", None, None),
            P("row", "col", None, None),
        ),
        out_specs=P("row", "col", None, None),
        check_vma=False,
    )
```

profile of v0, /device:TPU:1, one launch (start us, length us, event | category | flops | bytes accessed | tf_op | source)
XLA Modules:
  0.0 409.5 jit_solution(13803242583573978467)
XLA Ops:
  6.5 0.7 all-gather.2.cloned.1.call-update
  7.6 90.2 %all-gather.2.cloned.1.call-done = f32[2,32,256,256]{3,2,1,0:T(8,128)} async-done(((f32[2,4,256,256]{3,2,1,0:T(8,128)}), f32[2,32,256,256]{3,2,1,0:T(8,128)}) %all-gather.2.cloned.1.call-update) | async-done | bytes 16777232 | tf_op jit(solution)/shard_map/all_gather | solution.py:29
  97.9 7.8 %broadcast_in_dim.2 = f32[64,256,256]{2,1,0:T(8,128)} broadcast(f32[]{:T(128)} %constant.72.clone.1), dimensions={} | broadcast | bytes 16777220 | tf_op jit(solution)/shard_map/broadcast_in_dim | solution.py:47
  105.6 74.2 %while.10 = (s32[]{:T(128)}, f32[64,256,256]{2,1,0:T(8,128)}, s32[4,8]{1,0:T(4,128)S(1)}, s32[4,8]{1,0:T(4,128)S(1)}, f32[4,256,256]{2,1,0:T(8,128)S(1)}, /*inde...) while((s32[]{:T(128)}, f32[64,256,256]{2,1,0:T(8,128)}, s32[4,8]{1,0:T(4,128)S(1)}, ...), condition=%wide.region_2.3_spmd, body=%wide.region_0.2_spmd.sunk | while | flops 1611139200 | bytes 20980156 | solution.py:49
  105.7 2.0 gather_fusion
  107.7 7.8 %gather_fusion.1 = f32[8,256,256]{2,1,0:T(8,128)} fusion(f32[64,256,256]{2,1,0:T(8,128)} %get-tuple-element.133, s32[1024]{0:T(1024)S(1)} %pad_clamp_fusion.5), kind=kCustom, calls=%fused_computation.1.clone.1 | custom fusion | bytes 4194336 | tf_op jit(solution)/shard_map/while/body/eval_jaxpr/gather | solution.py:41
  115.5 4.3 %fusion.34 = f32[8,256,256]{2,1,0:T(8,128)S(1)} fusion(f32[8,256,256]{2,1,0:T(8,128)} %gather_fusion, f32[8,256,256]{2,1,0:T(8,128)} %gather_fusion.1), kind=kOutput, calls=%fused_computation.55.clone.1 | convolution fusion | flops 1610612736 | bytes 6291456 | tf_op jit(solution)/shard_map/while/body/eval_jaxpr/bxy,byz->bxz/dot_general | solution.py:38
  119.8 4.4 %scatter_fusion = f32[64,256,256]{2,1,0:T(8,128)} fusion(f32[64,256,256]{2,1,0:T(8,128)} %get-tuple-element.120, s32[8]{0:T(128)S(1)} %get-tuple-element.109, f32[8,256,256]{2,1,0:T(8,128)S(1)} %fusion.34), kind=kCustom, calls=%fused_computation.2.clone.1 | custom fusion | flops 524288 | bytes 6291488 | tf_op jit(solution)/shard_map/while/body/eval_jaxpr/scatter-add | solution.py:45
  124.2 2.0 gather_fusion
  126.2 7.8 %gather_fusion.1 = f32[8,256,256]{2,1,0:T(8,128)} fusion(f32[64,256,256]{2,1,0:T(8,128)} %get-tuple-element.133, s32[1024]{0:T(1024)S(1)} %pad_clamp_fusion.5), kind=kCustom, calls=%fused_computation.1.clone.1 | custom fusion | bytes 4194336 | tf_op jit(solution)/shard_map/while/body/eval_jaxpr/gather | solution.py:41
  134.0 4.3 %fusion.34 = f32[8,256,256]{2,1,0:T(8,128)S(1)} fusion(f32[8,256,256]{2,1,0:T(8,128)} %gather_fusion, f32[8,256,256]{2,1,0:T(8,128)} %gather_fusion.1), kind=kOutput, calls=%fused_computation.55.clone.1 | convolution fusion | flops 1610612736 | bytes 6291456 | tf_op jit(solution)/shard_map/while/body/eval_jaxpr/bxy,byz->bxz/dot_general | solution.py:38
  138.3 4.4 %scatter_fusion = f32[64,256,256]{2,1,0:T(8,128)} fusion(f32[64,256,256]{2,1,0:T(8,128)} %get-tuple-element.120, s32[8]{0:T(128)S(1)} %get-tuple-element.109, f32[8,256,256]{2,1,0:T(8,128)S(1)} %fusion.34), kind=kCustom, calls=%fused_computation.2.clone.1 | custom fusion | flops 524288 | bytes 6291488 | tf_op jit(solution)/shard_map/while/body/eval_jaxpr/scatter-add | solution.py:45
  142.8 2.0 gather_fusion
  144.8 7.8 %gather_fusion.1 = f32[8,256,256]{2,1,0:T(8,128)} fusion(f32[64,256,256]{2,1,0:T(8,128)} %get-tuple-element.133, s32[1024]{0:T(1024)S(1)} %pad_clamp_fusion.5), kind=kCustom, calls=%fused_computation.1.clone.1 | custom fusion | bytes 4194336 | tf_op jit(solution)/shard_map/while/body/eval_jaxpr/gather | solution.py:41
  152.6 4.3 %fusion.34 = f32[8,256,256]{2,1,0:T(8,128)S(1)} fusion(f32[8,256,256]{2,1,0:T(8,128)} %gather_fusion, f32[8,256,256]{2,1,0:T(8,128)} %gather_fusion.1), kind=kOutput, calls=%fused_computation.55.clone.1 | convolution fusion | flops 1610612736 | bytes 6291456 | tf_op jit(solution)/shard_map/while/body/eval_jaxpr/bxy,byz->bxz/dot_general | solution.py:38
  156.9 4.4 %scatter_fusion = f32[64,256,256]{2,1,0:T(8,128)} fusion(f32[64,256,256]{2,1,0:T(8,128)} %get-tuple-element.120, s32[8]{0:T(128)S(1)} %get-tuple-element.109, f32[8,256,256]{2,1,0:T(8,128)S(1)} %fusion.34), kind=kCustom, calls=%fused_computation.2.clone.1 | custom fusion | flops 524288 | bytes 6291488 | tf_op jit(solution)/shard_map/while/body/eval_jaxpr/scatter-add | solution.py:45
  161.3 2.0 gather_fusion
  163.3 7.8 %gather_fusion.1 = f32[8,256,256]{2,1,0:T(8,128)} fusion(f32[64,256,256]{2,1,0:T(8,128)} %get-tuple-element.133, s32[1024]{0:T(1024)S(1)} %pad_clamp_fusion.5), kind=kCustom, calls=%fused_computation.1.clone.1 | custom fusion | bytes 4194336 | tf_op jit(solution)/shard_map/while/body/eval_jaxpr/gather | solution.py:41
  171.2 4.3 %fusion.34 = f32[8,256,256]{2,1,0:T(8,128)S(1)} fusion(f32[8,256,256]{2,1,0:T(8,128)} %gather_fusion, f32[8,256,256]{2,1,0:T(8,128)} %gather_fusion.1), kind=kOutput, calls=%fused_computation.55.clone.1 | convolution fusion | flops 1610612736 | bytes 6291456 | tf_op jit(solution)/shard_map/while/body/eval_jaxpr/bxy,byz->bxz/dot_general | solution.py:38
  175.5 4.4 %scatter_fusion = f32[64,256,256]{2,1,0:T(8,128)} fusion(f32[64,256,256]{2,1,0:T(8,128)} %get-tuple-element.120, s32[8]{0:T(128)S(1)} %get-tuple-element.109, f32[8,256,256]{2,1,0:T(8,128)S(1)} %fusion.34), kind=kCustom, calls=%fused_computation.2.clone.1 | custom fusion | flops 524288 | bytes 6291488 | tf_op jit(solution)/shard_map/while/body/eval_jaxpr/scatter-add | solution.py:45
  179.9 0.6 copy-done.3
  180.5 0.6 dynamic-slice
  181.7 218.7 %all-reduce.3.cloned.1.call-done = f32[2,32,256,256]{3,2,1,0:T(8,128)} async-done(((f32[2,32,256,256]{3,2,1,0:T(8,128)}), f32[2,32,256,256]{3,2,1,0:T(8,128)}) %all-reduce.3.cloned.1.call-update) | async-done | bytes 16777232
  400.4 2.3 dynamic-slice_add_fusion
  (32 shorter events, 0.5 us)
Async XLA Ops:
  6.5 0.8 copy-start.2
  6.5 91.3 %all-gather.2.cloned.1.call-start = ((), (), s32[]{:S(2)}) async-start(), calls=%async_computation | async-start | bytes 18874368 | tf_op jit(solution)/shard_map/all_gather | solution.py:29
  7.3 393.1 %all-reduce.3.cloned.1.call-start = ((), (), s32[]{:S(2)}) async-start(), calls=%async_computation.1 | async-start | bytes 33554432
  97.9 7.8 %copy-start = (f32[2,2,256,256]{3,2,1,0:T(8,128)S(1)}, f32[2,2,256,256]{3,2,1,0:T(8,128)}, u32[]{:S(2)}) copy-start(f32[2,2,256,256]{3,2,1,0:T(8,128)} %param.6) | copy-start | bytes 3145732
  179.8 0.7 copy-start.3
  179.8 220.5 %copy-start.1 = (f32[2,2,256,256]{3,2,1,0:T(8,128)S(1)}, f32[2,2,256,256]{3,2,1,0:T(8,128)}, u32[]{:S(2)}) copy-start(f32[2,2,256,256]{3,2,1,0:T(8,128)} %param.8) | copy-start | bytes 3145732
Sparse Core Ops, SparseCore 0:
  9.1 88.7 all-gather.1
  180.0 220.3 all-reduce.2
where the time goes:
time: 410 us
  waiting for transfers between devices  310 us (76%)
  local copies, waits for them, and re-layouts  48.5 us (12%)
  other arithmetic  20 us (5%)
  matrix products  17.2 us (4%)
  between operations  14.1 us (3%)
    unnamed x3, waiting for transfers between devices  219 us
    all_gather x1, waiting for transfers between devices, on_device(): gathered = lax.all_gather(int_tiles, 'row', axis=1, tiled=True)  90.2 us
    gather x4, local copies, waits for them, and re-layouts, add_block(): int_flat[int_pick]  31.3 us
    scatter-add x4, other arithmetic, add_block(): return (partial_value.at[target_pick].add(products), None)  17.5 us
    dot_general x4, matrix products, add_block(): jnp.einsum('bxy,byz->bxz', amp_flat[amp_pick], int_flat[int_pick], precis...  17.2 us
  transfers between devices with their start and end apart: 2, of which 2 were waited for; matrix products, arithmetic and copies ran while one was open for 0% of the time, Pallas kernels for 0%

commit v1 on v0

--- a/solution.py
+++ b/solution.py
@@ -2,6 +2,7 @@
 import jax.numpy as jnp
 from jax import lax
 from jax.sharding import PartitionSpec as P
+from jax.lax import all_to_all, axis_size
 
 
 def on_device(amp_tiles, int_tiles, resid_init, triples):
@@ -26,7 +27,10 @@
     res_col = res_ids % all_k
     amp_index = amp_occ * vir_blocks + amp_vir
     int_index = int_vir * all_k + int_col
-    gathered = lax.all_gather(int_tiles, "row", axis=1, tiled=True)
+    plan_notes = lambda slab_in: jnp.concatenate(
+        all_to_all(jnp.stack([slab_in for _ in range(axis_size("row"))]), "row", 0, 0), axis=1
+    )
+    gathered = plan_notes(int_tiles)
     amp_flat = amp_tiles.reshape(-1, width, width)
     int_flat = gathered.reshape(-1, width, width)
     target = res_occ * all_k + res_col

time: 410 us -> 530 us (1.29)
  waiting for transfers between devices: 310 us -> 402 us
  local copies, waits for them, and re-layouts: 48.5 us -> 69.4 us
  starting transfers between devices: 0.04 us -> 7.18 us
    all_to_all x0 -> x1, waiting for transfers between devices: none -> 183 us  [on_device(): all_to_all(jnp.stack([slab_in for _ in range(axis_size('row'))]), 'row',...]
    all_gather x1 -> x0, waiting for transfers between devices: 90.2 us -> none  [on_device(): gathered = lax.all_gather(int_tiles, 'row', axis=1, tiled=True)]
    all_to_all x0 -> x1, local copies, waits for them, and re-layouts: none -> 11.5 us  [on_device(): all_to_all(jnp.stack([slab_in for _ in range(axis_size('row'))]), 'row',...]
    another operation x0 -> x1, local copies, waits for them, and re-layouts: none -> 9.48 us  [on_device(): jnp.stack([slab_in for _ in range(axis_size('row'))])]
    all_to_all x0 -> x1, starting transfers between devices: none -> 7.18 us  [on_device(): all_to_all(jnp.stack([slab_in for _ in range(axis_size('row'))]), 'row',...]
    unnamed x3 -> x2, waiting for transfers between devices: 219 us -> 219 us
where the time goes in v1:
time: 530 us
  waiting for transfers between devices  402 us (76%)
  local copies, waits for them, and re-layouts  69.4 us (13%)
  other arithmetic  20 us (4%)
  matrix products  17.2 us (3%)
  between operations  14.1 us (3%)
  starting transfers between devices  7.18 us (1%)
    unnamed x2, waiting for transfers between devices  219 us
    all_to_all x1, waiting for transfers between devices, on_device(): all_to_all(jnp.stack([slab_in for _ in range(axis_size('row'))]), 'row',...  183 us
    gather x4, local copies, waits for them, and re-layouts, add_block(): int_flat[int_pick]  31.3 us
    scatter-add x4, other arithmetic, add_block(): return (partial_value.at[target_pick].add(products), None)  17.5 us
    dot_general x4, matrix products, add_block(): jnp.einsum('bxy,byz->bxz', amp_flat[amp_pick], int_flat[int_pick], precis...  17.2 us
    all_to_all x1, local copies, waits for them, and re-layouts, on_device(): all_to_all(jnp.stack([slab_in for _ in range(axis_size('row'))]), 'row',...  11.5 us
  transfers between devices with their start and end apart: 2, of which 2 were waited for; matrix products, arithmetic and copies ran while one was open for 0% of the time, Pallas kernels for 0%

profile of v1, /device:TPU:1, one launch (start us, length us, event | category | flops | bytes accessed | tf_op | source)
XLA Modules:
  0.0 529.7 jit_solution(15877022099210956440)
XLA Ops:
  6.5 9.5 %stack.2 = f32[8,2,4,256,256]{4,3,2,1,0:T(8,128)} broadcast(f32[2,4,256,256]{3,2,1,0:T(8,128)} %param.7), dimensions={1,2,3,4} | broadcast | bytes 18874368 | tf_op jit(solution)/shard_map/stack | solution.py:31
  16.0 7.2 %all-to-all-start = ((f32[8,2,4,256,256]{4,3,2,1,0:T(8,128)}), f32[8,2,4,256,256]{4,3,2,1,0:T(8,128)}, u32[]{:S(2)}, u32[]{:S(2)}) async-start(f32[8,2,4,256,256]{4,3,2,1,0:T(8,128)} %stack.2), calls=%async_computation | async-start | bytes 33554432 | tf_op jit(solution)/shard_map/all_to_all | solution.py:31
  23.5 183.0 %all-to-all-done = f32[8,2,4,256,256]{4,3,2,1,0:T(8,128)} async-done(((f32[8,2,4,256,256]{4,3,2,1,0:T(8,128)}), f32[8,2,4,256,256]{4,3,2,1,0:T(8,128)}, u32[]{:S(2)}, u32[]{:S(2)}) %all-to-all-start) | async-done | bytes 16777248 | tf_op jit(solution)/shard_map/all_to_all | solution.py:31
  206.5 11.5 %copy.5 = f32[8,2,4,256,256]{4,3,2,0,1:T(8,128)} copy(f32[8,2,4,256,256]{4,3,2,1,0:T(8,128)} %all-to-all-done) | data formatting | bytes 33554432 | tf_op jit(solution)/shard_map/all_to_all | solution.py:31
  218.0 7.8 %broadcast_in_dim.2 = f32[64,256,256]{2,1,0:T(8,128)} broadcast(f32[]{:T(128)} %constant.72.clone.1), dimensions={} | broadcast | bytes 16777220 | tf_op jit(solution)/shard_map/broadcast_in_dim | solution.py:51
  225.8 74.2 %while.10 = (s32[]{:T(128)}, f32[64,256,256]{2,1,0:T(8,128)}, s32[4,8]{1,0:T(4,128)S(1)}, s32[4,8]{1,0:T(4,128)S(1)}, f32[4,256,256]{2,1,0:T(8,128)S(1)}, /*inde...) while((s32[]{:T(128)}, f32[64,256,256]{2,1,0:T(8,128)}, s32[4,8]{1,0:T(4,128)S(1)}, ...), condition=%wide.region_2.3_spmd, body=%wide.region_0.2_spmd.sunk | while | flops 1611139200 | bytes 20980156 | solution.py:53
  225.8 2.0 gather_fusion
  227.8 7.8 %gather_fusion.1 = f32[8,256,256]{2,1,0:T(8,128)} fusion(f32[64,256,256]{2,1,0:T(8,128)} %get-tuple-element.133, s32[1024]{0:T(1024)S(1)} %pad_clamp_fusion.5), kind=kCustom, calls=%fused_computation.1.clone.1 | custom fusion | bytes 4194336 | tf_op jit(solution)/shard_map/while/body/eval_jaxpr/gather | solution.py:45
  235.6 4.3 fusion.34
  240.0 4.4 scatter_fusion
  244.4 2.0 gather_fusion
  246.4 7.8 %gather_fusion.1 = f32[8,256,256]{2,1,0:T(8,128)} fusion(f32[64,256,256]{2,1,0:T(8,128)} %get-tuple-element.133, s32[1024]{0:T(1024)S(1)} %pad_clamp_fusion.5), kind=kCustom, calls=%fused_computation.1.clone.1 | custom fusion | bytes 4194336 | tf_op jit(solution)/shard_map/while/body/eval_jaxpr/gather | solution.py:45
  254.2 4.3 fusion.34
  258.5 4.4 scatter_fusion
  263.0 2.0 gather_fusion
  265.0 7.8 %gather_fusion.1 = f32[8,256,256]{2,1,0:T(8,128)} fusion(f32[64,256,256]{2,1,0:T(8,128)} %get-tuple-element.133, s32[1024]{0:T(1024)S(1)} %pad_clamp_fusion.5), kind=kCustom, calls=%fused_computation.1.clone.1 | custom fusion | bytes 4194336 | tf_op jit(solution)/shard_map/while/body/eval_jaxpr/gather | solution.py:45
  272.8 4.3 fusion.34
  277.1 4.4 scatter_fusion
  281.5 2.0 gather_fusion
  283.5 7.8 %gather_fusion.1 = f32[8,256,256]{2,1,0:T(8,128)} fusion(f32[64,256,256]{2,1,0:T(8,128)} %get-tuple-element.133, s32[1024]{0:T(1024)S(1)} %pad_clamp_fusion.5), kind=kCustom, calls=%fused_computation.1.clone.1 | custom fusion | bytes 4194336 | tf_op jit(solution)/shard_map/while/body/eval_jaxpr/gather | solution.py:45
  291.3 4.3 fusion.34
  295.6 4.4 scatter_fusion
  301.9 218.6 %all-reduce.3.cloned.1.call-done = f32[2,32,256,256]{3,2,1,0:T(8,128)} async-done(((f32[2,32,256,256]{3,2,1,0:T(8,128)}), f32[2,32,256,256]{3,2,1,0:T(8,128)}) %all-reduce.3.cloned.1.call-update) | async-done | bytes 16777232
  520.5 2.3 dynamic-slice_add_fusion
  (33 shorter events, 1.7 us)
Async XLA Ops:
  16.0 7.2 %copy-start.2 = (s32[1,1,3,32]{3,1,2,0:T(1,128)S(1)}, s32[1,1,3,32]{3,1,2,0:T(1,128)}, u32[]{:S(2)}) copy-start(s32[1,1,3,32]{3,1,2,0:T(1,128)} %param.9) | copy-start | bytes 1156
  16.0 190.5 %all-to-all-start = ((f32[8,2,4,256,256]{4,3,2,1,0:T(8,128)}), f32[8,2,4,256,256]{4,3,2,1,0:T(8,128)}, u32[]{:S(2)}, u32[]{:S(2)}) async-start(f32[8,2,4,256,256]{4,3,2,1,0:T(8,128)} %stack.2), calls=%async_computation | async-start | bytes 33554432 | tf_op jit(solution)/shard_map/all_to_all | solution.py:31
  23.2 497.3 %all-reduce.3.cloned.1.call-start = ((), (), s32[]{:S(2)}) async-start(), calls=%async_computation.1 | async-start | bytes 33554432
  218.0 7.8 %copy-start = (f32[2,2,256,256]{3,2,1,0:T(8,128)S(1)}, f32[2,2,256,256]{3,2,1,0:T(8,128)}, u32[]{:S(2)}) copy-start(f32[2,2,256,256]{3,2,1,0:T(8,128)} %param.6) | copy-start | bytes 3145732
  300.0 0.7 copy-start.3
  300.0 220.5 %copy-start.1 = (f32[2,2,256,256]{3,2,1,0:T(8,128)S(1)}, f32[2,2,256,256]{3,2,1,0:T(8,128)}, u32[]{:S(2)}) copy-start(f32[2,2,256,256]{3,2,1,0:T(8,128)} %param.8) | copy-start | bytes 3145732
Sparse Core Ops, SparseCore 0:
  300.1 220.3 all-reduce.2
